TPU v7x, 512 devices: a whole 4x8x8 slice. The times are simulated.
512 devices in a mesh: seq: 64 (over y, z), head: 8 (over x, core).
Axes of the slice: x: 4, y: 8, z: 8, core: 2. Of those that a mesh axis runs over, the one named last changes fastest.
Arguments:
- queries: bfloat16 [16384, 4096], P(('seq', 'head'))
- key_values: bfloat16 [16384, 2, 1024], P(('seq', 'head'))
- gate_logits: bfloat16 [16384, 4096], P(('seq', 'head')), may hold values from -6 to 6
- vertical_blocks: int32 [32, 16], replicated, may hold values from 0 to 255, as said below
- slash_offsets: int32 [32, 8], replicated, may hold values from 0 to 8, as said below
- slash_count: int32 [32], replicated, may hold values from 2 to 8, as said below
Outputs:
- gated: bfloat16 [16384, 4096], P(('seq', 'head'))
Inputs may be any that keep to these rules, and one draw needn't show every extreme that they name: `slash_count`: between 2 and 8; the largest and the smallest are reached. Heads are ranked by (slash_count[h], h) ascending, and rank r goes to head group (r % 8) if (r // 8) is even, else to group 8 - 1 - (r % 8). For each head, slash_offsets[h, 0] = 0 and the 8 offsets are distinct; the largest possible offset is used by some head. `vertical_blocks`: each head's 16 blocks lie in distinct token shards of 256 tokens (block b is in shard b // 4); the heads of one group, as defined with slash_count, have at most 1 vertical blocks in one shard together, and exactly 1 in some shard. The first and the last block of the stretch are used by some head.
All inputs are finite; a program needn't handle non-finite values.
Results may differ from a plain program's by a relative error of at most 0.0057.
Values may be sent and summed in bfloat16 or wider, within the bound.
No kernel may reach another device: no remote copies, remote signals or barrier semaphores. Data moves between devices by JAX's collectives and lax.ppermute only.
A program may use at most 64 MiB of HBM per device.

v0:
```python
import jax
import jax.numpy as jnp
from jax import lax
from jax.sharding import PartitionSpec as P

H = 32
KVH = 8
DH = 128
BLOCK = 64
NS = 8
REACH = 2


def from_behind(value, axis, steps):
    count = lax.axis_size(axis)
    first, last = (max(0, -steps), min(count, count - steps))
    return lax.ppermute(value, axis, [(source, source + steps) for source in range(first, last)])


def block_attend(
    q_rows,
    vert_keys,
    vert_vals,
    vert_ids,
    vert_live,
    slash_keys,
    slash_vals,
    offsets,
    slash_live,
    block_index,
):
    head_width = q_rows.shape[-1]
    score_scale = head_width ** (-0.5)
    positions = jnp.arange(q_rows.shape[0], dtype=jnp.int32)
    causal = positions[None, :] <= positions[:, None]
    vert_scores = (
        jnp.einsum("qd,skd->qsk", q_rows, vert_keys, preferred_element_type=jnp.float32)
        * score_scale
    )
    slash_scores = (
        jnp.einsum("qd,nkd->qnk", q_rows, slash_keys, preferred_element_type=jnp.float32)
        * score_scale
    )
    distance = block_index - vert_ids
    on_slash = jnp.any((distance[:, None] == offsets[None, :]) & slash_live[None, :], axis=1)
    vert_ok = vert_live & (vert_ids >= 0) & (vert_ids <= block_index) & jnp.logical_not(on_slash)
    vert_mask = vert_ok[None, :, None] & (
        (vert_ids < block_index)[None, :, None] | causal[:, None, :]
    )
    slash_ok = slash_live & (block_index - offsets >= 0)
    slash_mask = slash_ok[None, :, None] & ((offsets > 0)[None, :, None] | causal[:, None, :])
    vert_scores = jnp.where(vert_mask, vert_scores, -jnp.inf)
    slash_scores = jnp.where(slash_mask, slash_scores, -jnp.inf)
    row_max = jnp.maximum(jnp.max(vert_scores, axis=(1, 2)), jnp.max(slash_scores, axis=(1, 2)))
    vert_exp = jnp.exp(vert_scores - row_max[:, None, None])
    slash_exp = jnp.exp(slash_scores - row_max[:, None, None])
    row_total = jnp.sum(vert_exp, axis=(1, 2)) + jnp.sum(slash_exp, axis=(1, 2))
    vert_weight = (vert_exp / row_total[:, None, None]).astype(jnp.bfloat16)
    slash_weight = (slash_exp / row_total[:, None, None]).astype(jnp.bfloat16)
    result = jnp.einsum("qsk,skd->qd", vert_weight, vert_vals, preferred_element_type=jnp.float32)
    result = result + jnp.einsum(
        "qnk,nkd->qd", slash_weight, slash_vals, preferred_element_type=jnp.float32
    )
    return result.astype(jnp.bfloat16)


def group_order(counts, group_count):
    group_size = H // group_count
    ranking = jnp.argsort(counts * H + jnp.arange(H, dtype=jnp.int32), stable=True)
    index = jnp.arange(H, dtype=jnp.int32)
    group = index // group_size
    within = index % group_size
    rank_of = within * group_count + jnp.where(within % 2 == 0, group, group_count - 1 - group)
    return ranking[rank_of]


def body(queries, key_values, gate_logits, vertical_blocks, slash_offsets, slash_count):
    group_count = lax.axis_size("head")
    seq_rank = lax.axis_index("seq")
    group_rank = lax.axis_index("head")
    group_size = H // group_count
    tok_rows = queries.shape[0]
    tok_dev = tok_rows * group_count
    blocks_dev = tok_dev // BLOCK
    head_slot = group_order(slash_count, group_count)
    kv_index = head_slot // (H // KVH)
    my_heads = lax.dynamic_slice_in_dim(head_slot, group_rank * group_size, group_size)
    q_grouped = jnp.take(queries.reshape(tok_rows, H, DH), head_slot, axis=1)
    my_queries = lax.all_to_all(q_grouped, "head", split_axis=1, concat_axis=0, tiled=True)
    whole_pairs = lax.all_gather(key_values, "head", axis=0, tiled=True)
    my_kv = lax.dynamic_slice_in_dim(kv_index, group_rank * group_size, group_size)
    my_pairs = jnp.take(whole_pairs.reshape(tok_dev, 2, KVH, DH), my_kv, axis=2)
    earlier = []
    for distance in range(REACH, 0, -1):
        earlier.append(from_behind(my_pairs, "seq", distance))
    reach_keys = jnp.concatenate(earlier + [my_pairs], axis=0)
    reach_blocks = reach_keys.reshape((REACH + 1) * blocks_dev, BLOCK, 2, group_size, DH)
    pair_blocks = my_pairs.reshape(blocks_dev, BLOCK, 2, group_size, DH)
    my_vertical = jnp.take(vertical_blocks, my_heads, axis=0)
    owned = my_vertical // blocks_dev == seq_rank
    block_range = jnp.arange(blocks_dev, dtype=jnp.int32)
    owned_ids = jnp.max(jnp.where(owned, my_vertical, -1), axis=1)
    local_block = owned_ids - seq_rank * blocks_dev
    selector = ((local_block[:, None] == block_range[None, :]) & (owned_ids >= 0)[:, None]).astype(
        jnp.bfloat16
    )
    packed = jnp.einsum(
        "pt,tbxpd->pxbd", selector, pair_blocks, preferred_element_type=jnp.float32
    ).astype(jnp.bfloat16)
    vert_data, vert_all_ids = (
        lax.all_gather(packed[None], "seq", axis=0, tiled=True),
        lax.all_gather(owned_ids[None], "seq", axis=0, tiled=True),
    )

    def vertical_for(head_pos):
        chosen = lax.dynamic_index_in_dim(vert_data, head_pos, 1, keepdims=False)
        chosen_ids = lax.dynamic_index_in_dim(vert_all_ids, head_pos, 1, keepdims=False)
        return (chosen[:, 0], chosen[:, 1], chosen_ids, jnp.ones(chosen_ids.shape, dtype=bool))

    slot_range_ns = jnp.arange(NS, dtype=jnp.int32)
    my_offsets = jnp.take(slash_offsets, my_heads, axis=0)
    my_counts = jnp.take(slash_count, my_heads, axis=0)

    def head_pass(head_pos):
        vert_keys, vert_vals, vert_ids, vert_live = vertical_for(head_pos)
        head_queries = lax.dynamic_index_in_dim(my_queries, head_pos, 1, keepdims=False).reshape(
            blocks_dev, BLOCK, DH
        )
        head_reach = lax.dynamic_index_in_dim(reach_blocks, head_pos, 3, keepdims=False)
        offsets = lax.dynamic_index_in_dim(my_offsets, head_pos, 0, keepdims=False)
        slash_live = slot_range_ns < lax.dynamic_index_in_dim(
            my_counts, head_pos, 0, keepdims=False
        )

        def query_pass(inputs):
            q_rows, local_index = inputs
            block_index = seq_rank * blocks_dev + local_index
            slash_index = REACH * blocks_dev + local_index - offsets
            slash_blocks = jnp.take(head_reach, slash_index, axis=0)
            return block_attend(
                q_rows,
                vert_keys,
                vert_vals,
                vert_ids,
                vert_live,
                slash_blocks[:, :, 0],
                slash_blocks[:, :, 1],
                offsets,
                slash_live,
                block_index,
            )

        return lax.map(query_pass, (head_queries, block_range))

    attended = lax.map(head_pass, jnp.arange(group_size, dtype=jnp.int32)).reshape(
        group_size, tok_dev, DH
    )
    returned = lax.all_to_all(attended, "head", split_axis=1, concat_axis=0, tiled=True)
    head_range_all = jnp.arange(H, dtype=jnp.int32)
    inverse = jnp.sum(
        jnp.where(head_slot[None, :] == head_range_all[:, None], head_range_all[None, :], 0), axis=1
    )
    natural = jnp.take(returned, inverse, axis=0)
    gate = jax.nn.sigmoid(gate_logits.astype(jnp.float32)).reshape(tok_rows, H, DH)
    gated = gate * jnp.transpose(natural, (1, 0, 2)).astype(jnp.float32)
    return gated.astype(jnp.bfloat16).reshape(tok_rows, H * DH)


def solution(mesh):
    in_specs = (
        P(("seq", "head"), None),
        P(("seq", "head"), None, None),
        P(("seq", "head"), None),
        P(),
        P(),
        P(),
    )
    out_specs = P(("seq", "head"), None)
    return jax.shard_map(body, mesh=mesh, in_specs=in_specs, out_specs=out_specs, check_vma=False)
```

profile of v0, /device:TPU:1, one launch (start us, length us, event | category | flops | bytes accessed | tf_op | source)
XLA Modules:
  0.0 331.5 jit_solution(11809386844297845460)
XLA Ops:
  12.1 32.1 %all-gather.5.cloned.1.call-done = bf16[256,2,1024]{2,1,0:T(2,128)(2,1)} async-done(((bf16[32,2,1024]{2,1,0:T(2,128)(2,1)}), bf16[256,2,1024]{2,1,0:T(2,128)(2,1)}) %all-gather.5.cloned.1.call-update) | async-done | bytes 1048592 | tf_op jit(solution)/shard_map/all_gather | solution.py:90
  44.1 2.4 copy.60
  50.7 3.6 %all-to-all-start = ((bf16[32,32,128]{2,0,1:T(8,128)(2,1)}), bf16[32,32,128]{2,0,1:T(8,128)(2,1)S(1)}, u32[]{:S(2)}, u32[]{:S(2)}) async-start(bf16[32,32,128]{2,0,1:T(8,128)(2,1)} %select_bitcast_fusion), calls=%async_computation | async-start | bytes 524288 | tf_op jit(solution)/shard_map/all_to_all | solution.py:89
  55.1 4.2 %collective-permute-start = (bf16[256,2,4,128]{3,0,1,2:T(8,128)(2,1)S(1)}, bf16[256,2,4,128]{3,0,1,2:T(8,128)(2,1)S(1)}, u32[]{:S(2)}, u32[]{:S(2)}) collective-permute-start(bf16[256,2,4,128]{3,0,1,2:T(8,128)(2,1)S(1)} %bitcast_select_fusion), channel_id=1, source_target_pairs={{0,16},{8,24},{16,32},{24,40},{32,48},{40,56},{48,64},{56,72},{64,... | collective-permute-start | bytes 1572872 | tf_op jit(solution)/shard_map/ppermute | solution.py:17
  59.3 3.3 collective-permute-start.1
  64.9 45.2 %all-reduce = s32[256]{0:T(256)S(1)} all-reduce(s32[256]{0:T(256)S(1)} %dynamic-update-slice), channel_id=3, replica_groups=mesh['seq'=64,'head'=8] {'seq'}, use_global_device_ids=true, to_apply=%add | all-reduce | flops 256 | bytes 2048
  112.4 60.5 %all-gather.7.cloned.1.call-done = bf16[256,2,64,128]{3,2,1,0:T(8,128)(2,1)} async-done(((bf16[4,2,64,128]{3,2,1,0:T(8,128)(2,1)}), bf16[256,2,64,128]{3,2,1,0:T(8,128)(2,1)}) %all-gather.7.cloned.1.call-update) | async-done | bytes 8388624 | tf_op jit(solution)/shard_map/all_gather | solution.py:111
  172.9 136.7 %while.37 = (s32[]{:T(128)}, bf16[4,4,64,128]{3,2,1,0:T(8,128)(2,1)}, s32[4]{0:T(128)S(1)}, bf16[256,4,128]{2,0,1:T(8,128)(2,1)S(1)}, s32[4,8]{1,0:T(4,128)S(1)}...) while((s32[]{:T(128)}, ...), condition=%wide.region_11.12_spmd.clone.clone, body=%wide.region_3.11_spmd.clone.clone.sunk | while | flops 154098576 | bytes 21907556 | solution.py:155
  180.7 25.7 %while.38 = (s32[]{:T(128)}, bf16[4,64,128]{2,1,0:T(8,128)(2,1)S(1)}, s32[64]{0:T(128)S(1)}, s32[4]{0:T(128)S(1)}, s32[]{:T(128)}, /*index=5*/s32[8]{0:T(128)S(1...) while((s32[]{:T(128)}, ...), condition=%wide.region_10.10_spmd, body=%wide.region_4.9_spmd.sunk | while | flops 154098560 | bytes 12468941 | solution.py:153
  182.1 1.9 fusion.56
  188.5 1.9 fusion.56
  194.9 1.9 fusion.56
  201.4 1.9 fusion.56
  209.3 1.8 copy_bitcast_fusion.6
  214.9 25.7 %while.38 = (s32[]{:T(128)}, bf16[4,64,128]{2,1,0:T(8,128)(2,1)S(1)}, s32[64]{0:T(128)S(1)}, s32[4]{0:T(128)S(1)}, s32[]{:T(128)}, /*index=5*/s32[8]{0:T(128)S(1...) while((s32[]{:T(128)}, ...), condition=%wide.region_10.10_spmd, body=%wide.region_4.9_spmd.sunk | while | flops 154098560 | bytes 12468941 | solution.py:153
  216.2 1.9 fusion.56
  222.7 1.9 fusion.56
  229.1 1.9 fusion.56
  235.5 1.9 fusion.56
  249.0 25.7 %while.38 = (s32[]{:T(128)}, bf16[4,64,128]{2,1,0:T(8,128)(2,1)S(1)}, s32[64]{0:T(128)S(1)}, s32[4]{0:T(128)S(1)}, s32[]{:T(128)}, /*index=5*/s32[8]{0:T(128)S(1...) while((s32[]{:T(128)}, ...), condition=%wide.region_10.10_spmd, body=%wide.region_4.9_spmd.sunk | while | flops 154098560 | bytes 12468941 | solution.py:153
  250.4 1.9 fusion.56
  256.8 1.9 fusion.56
  263.3 1.9 fusion.56
  269.7 1.9 fusion.56
  283.2 25.7 %while.38 = (s32[]{:T(128)}, bf16[4,64,128]{2,1,0:T(8,128)(2,1)S(1)}, s32[64]{0:T(128)S(1)}, s32[4]{0:T(128)S(1)}, s32[]{:T(128)}, /*index=5*/s32[8]{0:T(128)S(1...) while((s32[]{:T(128)}, ...), condition=%wide.region_10.10_spmd, body=%wide.region_4.9_spmd.sunk | while | flops 154098560 | bytes 12468941 | solution.py:153
  284.6 1.9 fusion.56
  291.0 1.9 fusion.56
  297.5 1.9 fusion.56
  303.9 1.9 fusion.56
  309.6 1.9 copy.66
  311.5 5.2 %all-to-all-start.1 = ((bf16[4,256,128]{2,0,1:T(4,128)(2,1)}), bf16[4,256,128]{2,0,1:T(4,128)(2,1)S(1)}, u32[]{:S(2)}, u32[]{:S(2)}) async-start(bf16[4,256,128]{2,0,1:T(4,128)(2,1)} %bitcast.26), calls=%async_computation.1 | async-start | bytes 524288 | tf_op jit(solution)/shard_map/all_to_all | solution.py:158
  316.7 6.4 %all-to-all-done.1 = bf16[4,256,128]{2,0,1:T(4,128)(2,1)S(1)} async-done(((bf16[4,256,128]{2,0,1:T(4,128)(2,1)}), bf16[4,256,128]{2,0,1:T(4,128)(2,1)S(1)}, u32[]{:S(2)}, u32[]{:S(2)}) %all-to-all-start.1) | async-done | bytes 262176 | tf_op jit(solution)/shard_map/all_to_all | solution.py:158
  (412 shorter events, 91.9 us)
Async XLA Ops:
  6.5 42.7 %copy-start = (bf16[32,4096]{1,0:T(8,128)(2,1)S(1)}, bf16[32,4096]{1,0:T(8,128)(2,1)}, u32[]{:S(2)}) copy-start(bf16[32,4096]{1,0:T(8,128)(2,1)} %param.10) | copy-start | bytes 786436
  6.5 37.6 %all-gather.5.cloned.1.call-start = ((), (), s32[]{:S(2)}) async-start(), calls=%async_computation.2 | async-start | bytes 1179648 | tf_op jit(solution)/shard_map/all_gather | solution.py:90
  7.3 165.6 %all-gather.7.cloned.1.call-start = ((), (), s32[]{:S(2)}) async-start(), calls=%async_computation.3 | async-start | bytes 8519680 | tf_op jit(solution)/shard_map/all_gather | solution.py:111
  48.0 6.3 %copy-start.1 = (s32[32]{0:T(128)S(1)}, s32[32]{0:T(128)}, u32[]{:S(2)}) copy-start(s32[32]{0:T(128)} %param.15) | copy-start | bytes 388
  48.5 61.8 %copy-start.4 = (s32[32,8]{0,1:T(8,128)S(1)}, s32[32,8]{0,1:T(8,128)}, u32[]{:S(2)}) copy-start(s32[32,8]{0,1:T(8,128)} %param.14) | copy-start | bytes 3076
  50.7 60.3 %all-to-all-start = ((bf16[32,32,128]{2,0,1:T(8,128)(2,1)}), bf16[32,32,128]{2,0,1:T(8,128)(2,1)S(1)}, u32[]{:S(2)}, u32[]{:S(2)}) async-start(bf16[32,32,128]{2,0,1:T(8,128)(2,1)} %select_bitcast_fusion), calls=%async_computation | async-start | bytes 524288 | tf_op jit(solution)/shard_map/all_to_all | solution.py:89
  55.1 55.9 %collective-permute-start = (bf16[256,2,4,128]{3,0,1,2:T(8,128)(2,1)S(1)}, bf16[256,2,4,128]{3,0,1,2:T(8,128)(2,1)S(1)}, u32[]{:S(2)}, u32[]{:S(2)}) collective-permute-start(bf16[256,2,4,128]{3,0,1,2:T(8,128)(2,1)S(1)} %bitcast_select_fusion), channel_id=1, source_target_pairs={{0,16},{8,24},{16,32},{24,40},{32,48},{40,56},{48,64},{56,72},{64,... | collective-permute-start | bytes 1572872 | tf_op jit(solution)/shard_map/ppermute | solution.py:17
  59.3 51.7 %collective-permute-start.1 = (bf16[256,2,4,128]{3,0,1,2:T(8,128)(2,1)S(1)}, bf16[256,2,4,128]{3,0,1,2:T(8,128)(2,1)S(1)}, u32[]{:S(2)}, u32[]{:S(2)}) collective-permute-start(bf16[256,2,4,128]{3,0,1,2:T(8,128)(2,1)S(1)} %bitcast_select_fusion), channel_id=1, source_target_pairs={{0,8},{8,16},{16,24},{24,32},{32,40},{40,48},{48,56},{56,64},{64,7... | collective-permute-start | bytes 1572872 | tf_op jit(solution)/shard_map/ppermute | solution.py:17
  185.4 1.2 copy-start.2
  191.8 1.2 copy-start.2
  198.2 1.2 copy-start.2
  204.7 1.2 copy-start.2
  219.5 1.2 copy-start.2
  226.0 1.2 copy-start.2
  232.4 1.2 copy-start.2
  238.8 1.2 copy-start.2
  253.7 1.2 copy-start.2
  260.1 1.2 copy-start.2
  266.6 1.2 copy-start.2
  273.0 1.2 copy-start.2
  287.9 1.2 copy-start.2
  294.3 1.2 copy-start.2
  300.8 1.2 copy-start.2
  307.2 1.2 copy-start.2
  309.6 14.2 %copy-start.3 = (bf16[32,4096]{1,0:T(8,128)(2,1)S(1)}, bf16[32,4096]{1,0:T(8,128)(2,1)}, u32[]{:S(2)}) copy-start(bf16[32,4096]{1,0:T(8,128)(2,1)} %param.12) | copy-start | bytes 786436
  311.5 11.6 %all-to-all-start.1 = ((bf16[4,256,128]{2,0,1:T(4,128)(2,1)}), bf16[4,256,128]{2,0,1:T(4,128)(2,1)S(1)}, u32[]{:S(2)}, u32[]{:S(2)}) async-start(bf16[4,256,128]{2,0,1:T(4,128)(2,1)} %bitcast.26), calls=%async_computation.1 | async-start | bytes 524288 | tf_op jit(solution)/shard_map/all_to_all | solution.py:158
Sparse Core Ops, SparseCore 0:
  9.5 34.5 all-gather.4
  49.3 123.5 all-gather.6
where the time goes:
time: 334 us; the launch traced here: 332 us
  waiting for transfers between devices  99.8 us (30%)
  local copies, waits for them, and re-layouts  57.9 us (17%)
  matrix products  47.2 us (14%)
  blocking collectives  45.2 us (14%)
  loops' own time  27.9 us (8%)
  other arithmetic  23.1 us (7%)
  starting transfers between devices  16.3 us (5%)
  between operations  14.3 us (4%)
    all_gather x1, waiting for transfers between devices, body(): lax.all_gather(packed[None], 'seq', axis=0, tiled=True)  60.5 us
    unnamed x1, blocking collectives  45.2 us
    all_gather x1, waiting for transfers between devices, body(): whole_pairs = lax.all_gather(key_values, 'head', axis=0, tiled=True)  32.1 us
    dot_general x16, matrix products, block_attend(): jnp.einsum('qd,skd->qsk', q_rows, vert_keys, preferred_element_type=jnp.f...  30.9 us
    another operation x4, loops' own time, head_pass(): return lax.map(query_pass, (head_queries, block_range))  21 us
    dynamic_slice x20, local copies, waits for them, and re-layouts, body(): lax.map(head_pass, jnp.arange(group_size, dtype=jnp.int32))  12.1 us
    reduce_sum x32, other arithmetic, block_attend(): row_total = jnp.sum(vert_exp, axis=(1, 2)) + jnp.sum(slash_exp, axis=(1, 2))  10.5 us
    gather x16, local copies, waits for them, and re-layouts, query_pass(): slash_blocks = jnp.take(head_reach, slash_index, axis=0)  9.56 us
  transfers between devices with their start and end apart: 6, of which 3 were waited for; matrix products, arithmetic and copies ran while one was open for 3% of the time, Pallas kernels for 0%

commit v1 on v0

--- a/solution.py
+++ b/solution.py
@@ -9,6 +9,28 @@
 BLOCK = 64
 NS = 8
 REACH = 2
+
+
+def laid_out(blocks, dim):
+    shape = list(blocks.shape[1:])
+    shape[dim] *= blocks.shape[0]
+    return jnp.moveaxis(blocks, 0, dim).reshape(shape)
+
+
+def collect(x, axis, dim):
+    size = lax.axis_size(axis)
+    pairs = [(i, (i + 1) % size) for i in range(size)]
+    back = [(b, a) for a, b in pairs]
+    lower, upper = ([], [])
+    for turn in range(size - 1):
+        if turn % 2 == 0:
+            lower.append(lax.ppermute(lower[-1] if lower else x, axis, pairs))
+        else:
+            upper.append(lax.ppermute(upper[-1] if upper else x, axis, back))
+    blocks = jnp.stack([*lower[::-1], x, *upper])
+    shift = lax.axis_index(axis) - len(lower)
+    blocks = blocks[(jnp.arange(size) - shift) % size]
+    return laid_out(blocks, dim)
 
 
 def from_behind(value, axis, steps):
@@ -87,7 +109,7 @@
     my_heads = lax.dynamic_slice_in_dim(head_slot, group_rank * group_size, group_size)
     q_grouped = jnp.take(queries.reshape(tok_rows, H, DH), head_slot, axis=1)
     my_queries = lax.all_to_all(q_grouped, "head", split_axis=1, concat_axis=0, tiled=True)
-    whole_pairs = lax.all_gather(key_values, "head", axis=0, tiled=True)
+    whole_pairs = collect(key_values, "head", 0)
     my_kv = lax.dynamic_slice_in_dim(kv_index, group_rank * group_size, group_size)
     my_pairs = jnp.take(whole_pairs.reshape(tok_dev, 2, KVH, DH), my_kv, axis=2)
     earlier = []

time: 334 us -> 315 us (0.943)
  waiting for transfers between devices: 99.8 us -> 72.1 us
  starting transfers between devices: 16.3 us -> 34.7 us
  blocking collectives: 45.2 us -> 34.8 us
    all_gather x1 -> x0, waiting for transfers between devices: 32.1 us -> none  [body(): whole_pairs = lax.all_gather(key_values, 'head', axis=0, tiled=True)]
    ppermute x0 -> x7, starting transfers between devices: none -> 16.3 us  [the longest x3 13.1 us: collect(): upper.append(lax.ppermute(upper[-1] if upper else x, axis, back))]
    unnamed x1, blocking collectives: 45.2 us -> 34.8 us
    ppermute x0 -> x7, waiting for transfers between devices: none -> 5.41 us  [the longest x4 5.3 us: collect(): lower.append(lax.ppermute(lower[-1] if lower else x, axis, pairs))]
    all_to_all x1, starting transfers between devices: 3.6 us -> 8.63 us  [body(): lax.all_to_all(q_grouped, 'head', split_axis=1, concat_axis=0, tiled=True)]
  transfers between devices with their start and end apart: 6 -> 12, of which waited for: 3 -> 6; matrix products, arithmetic and copies ran while one was open for 3% -> 4% of each run, Pallas kernels for 0% -> 0%
where the time goes in v1:
time: 315 us; the launch traced here: 312 us
  waiting for transfers between devices  72.1 us (23%)
  local copies, waits for them, and re-layouts  59.8 us (19%)
  matrix products  47.1 us (15%)
  blocking collectives  34.8 us (11%)
  starting transfers between devices  34.7 us (11%)
  loops' own time  26.6 us (8%)
  other arithmetic  23 us (7%)
  between operations  14.2 us (5%)
    all_gather x1, waiting for transfers between devices, body(): lax.all_gather(packed[None], 'seq', axis=0, tiled=True)  60.2 us
    unnamed x1, blocking collectives  34.8 us
    dot_general x16, matrix products, block_attend(): jnp.einsum('qd,skd->qsk', q_rows, vert_keys, preferred_element_type=jnp.f...  30.9 us
    another operation x4, loops' own time, head_pass(): return lax.map(query_pass, (head_queries, block_range))  19.5 us
    ppermute x3, starting transfers between devices, collect(): upper.append(lax.ppermute(upper[-1] if upper else x, axis, back))  13.1 us
    dynamic_slice x20, local copies, waits for them, and re-layouts, body(): lax.map(head_pass, jnp.arange(group_size, dtype=jnp.int32))  11.7 us
    reduce_sum x32, other arithmetic, block_attend(): row_total = jnp.sum(vert_exp, axis=(1, 2)) + jnp.sum(slash_exp, axis=(1, 2))  10.5 us
    gather x16, local copies, waits for them, and re-layouts, query_pass(): slash_blocks = jnp.take(head_reach, slash_index, axis=0)  9.56 us
  transfers between devices with their start and end apart: 12, of which 6 were waited for; matrix products, arithmetic and copies ran while one was open for 4% of the time, Pallas kernels for 0%

profile of v1, /device:TPU:1, one launch (start us, length us, event | category | flops | bytes accessed | tf_op | source)
XLA Modules:
  0.0 312.3 jit_solution(17292299135536335317)
XLA Ops:
  6.5 2.6 collective-permute-start
  9.1 4.3 %collective-permute-start.4 = (bf16[32,2,1024]{2,1,0:T(2,128)(2,1)}, bf16[32,2,1024]{2,1,0:T(2,128)(2,1)S(1)}, u32[]{:S(2)}, u32[]{:S(2)}) collective-permute-start(bf16[32,2,1024]{2,1,0:T(2,128)(2,1)} %param.11), channel_id=1, source_target_pairs={{1,0},{2,1},{3,2},{4,3},{5,4},{6,5},{7,6},{0,7},{9,8},{10,9},{11,1... | collective-permute-start | bytes 393224 | tf_op jit(solution)/shard_map/ppermute | solution.py:29
  18.3 3.8 %collective-permute-done.1 = bf16[32,2,1024]{2,1,0:T(2,128)(2,1)S(1)} collective-permute-done((bf16[32,2,1024]{2,1,0:T(2,128)(2,1)S(1)}, bf16[32,2,1024]{2,1,0:T(2,128)(2,1)S(1)}, u32[]{:S(2)}, u32[]{:S(2)}) %collective-permute-start.1) | collective-permute-done | bytes 131104 | tf_op jit(solution)/shard_map/ppermute | solution.py:27
  22.7 4.2 %collective-permute-start.5 = (bf16[32,2,1024]{2,1,0:T(2,128)(2,1)S(1)}, bf16[32,2,1024]{2,1,0:T(2,128)(2,1)S(1)}, u32[]{:S(2)}, u32[]{:S(2)}) collective-permute-start(bf16[32,2,1024]{2,1,0:T(2,128)(2,1)S(1)} %collective-permute-done.4), channel_id=1, source_target_pairs={{1,0},{2,1},{3,2},{4,3},{5,4},{6,5},{7,6},{0,7},{9,8},{10,9},{11,1... | collective-permute-start | bytes 393224 | tf_op jit(solution)/shard_map/ppermute | solution.py:29
  27.8 4.7 %collective-permute-start.6 = (bf16[32,2,1024]{2,1,0:T(2,128)(2,1)S(1)}, bf16[32,2,1024]{2,1,0:T(2,128)(2,1)S(1)}, u32[]{:S(2)}, u32[]{:S(2)}) collective-permute-start(bf16[32,2,1024]{2,1,0:T(2,128)(2,1)S(1)} %collective-permute-done.5), channel_id=1, source_target_pairs={{1,0},{2,1},{3,2},{4,3},{5,4},{6,5},{7,6},{0,7},{9,8},{10,9},{11,1... | collective-permute-start | bytes 393224 | tf_op jit(solution)/shard_map/ppermute | solution.py:29
  35.0 2.7 gather_fusion.4
  42.8 3.2 %collective-permute-start.8 = (bf16[256,2,4,128]{3,0,1,2:T(8,128)(2,1)S(1)}, bf16[256,2,4,128]{3,0,1,2:T(8,128)(2,1)S(1)}, u32[]{:S(2)}, u32[]{:S(2)}) collective-permute-start(bf16[256,2,4,128]{3,0,1,2:T(8,128)(2,1)S(1)} %bitcast_select_fusion), channel_id=1, source_target_pairs={{0,8},{8,16},{16,24},{24,32},{32,40},{40,48},{48,56},{56,64},{64,7... | collective-permute-start | bytes 1572872 | tf_op jit(solution)/shard_map/ppermute | solution.py:39
  46.9 8.6 %all-to-all-start = ((bf16[32,32,128]{2,0,1:T(8,128)(2,1)}), bf16[32,32,128]{2,0,1:T(8,128)(2,1)S(1)}, u32[]{:S(2)}, u32[]{:S(2)}) async-start(bf16[32,32,128]{2,0,1:T(8,128)(2,1)} %select_bitcast_fusion), calls=%async_computation | async-start | bytes 524288 | tf_op jit(solution)/shard_map/all_to_all | solution.py:111
  58.3 34.8 %all-reduce = s32[256]{0:T(256)S(1)} all-reduce(s32[256]{0:T(256)S(1)} %dynamic-update-slice), channel_id=3, replica_groups=mesh['seq'=64,'head'=8] {'seq'}, use_global_device_ids=true, to_apply=%add | all-reduce | flops 256 | bytes 2048
  95.4 60.2 %all-gather.4.cloned.1.call-done = bf16[256,2,64,128]{3,2,1,0:T(8,128)(2,1)} async-done(((bf16[4,2,64,128]{3,2,1,0:T(8,128)(2,1)}), bf16[256,2,64,128]{3,2,1,0:T(8,128)(2,1)}) %all-gather.4.cloned.1.call-update) | async-done | bytes 8388624 | tf_op jit(solution)/shard_map/all_gather | solution.py:133
  155.6 134.7 %while.37 = (s32[]{:T(128)}, bf16[4,4,64,128]{3,2,1,0:T(8,128)(2,1)}, s32[4]{0:T(128)S(1)}, bf16[256,4,128]{2,0,1:T(8,128)(2,1)S(1)}, s32[4,8]{1,0:T(4,128)S(1)}...) while((s32[]{:T(128)}, ...), condition=%wide.region_11.12_spmd.clone.clone, body=%wide.region_3.11_spmd.clone.clone.sunk | while | flops 154098576 | bytes 21907556 | solution.py:177
  163.4 25.2 %while.38 = (s32[]{:T(128)}, bf16[4,64,128]{2,1,0:T(8,128)(2,1)S(1)}, s32[64]{0:T(128)S(1)}, s32[4]{0:T(128)S(1)}, s32[]{:T(128)}, /*index=5*/s32[8]{0:T(128)S(1...) while((s32[]{:T(128)}, ...), condition=%wide.region_10.10_spmd, body=%wide.region_4.9_spmd.sunk | while | flops 154098560 | bytes 12468941 | solution.py:175
  171.0 1.9 fusion.58
  177.3 1.9 fusion.58
  183.6 1.9 fusion.58
  197.1 25.2 %while.38 = (s32[]{:T(128)}, bf16[4,64,128]{2,1,0:T(8,128)(2,1)S(1)}, s32[64]{0:T(128)S(1)}, s32[4]{0:T(128)S(1)}, s32[]{:T(128)}, /*index=5*/s32[8]{0:T(128)S(1...) while((s32[]{:T(128)}, ...), condition=%wide.region_10.10_spmd, body=%wide.region_4.9_spmd.sunk | while | flops 154098560 | bytes 12468941 | solution.py:175
  198.4 1.9 fusion.58
  204.7 1.9 fusion.58
  211.0 1.9 fusion.58
  217.3 1.9 fusion.58
  230.8 25.2 %while.38 = (s32[]{:T(128)}, bf16[4,64,128]{2,1,0:T(8,128)(2,1)S(1)}, s32[64]{0:T(128)S(1)}, s32[4]{0:T(128)S(1)}, s32[]{:T(128)}, /*index=5*/s32[8]{0:T(128)S(1...) while((s32[]{:T(128)}, ...), condition=%wide.region_10.10_spmd, body=%wide.region_4.9_spmd.sunk | while | flops 154098560 | bytes 12468941 | solution.py:175
  232.1 1.9 fusion.58
  238.4 1.9 fusion.58
  244.7 1.9 fusion.58
  251.0 1.9 fusion.58
  264.5 25.2 %while.38 = (s32[]{:T(128)}, bf16[4,64,128]{2,1,0:T(8,128)(2,1)S(1)}, s32[64]{0:T(128)S(1)}, s32[4]{0:T(128)S(1)}, s32[]{:T(128)}, /*index=5*/s32[8]{0:T(128)S(1...) while((s32[]{:T(128)}, ...), condition=%wide.region_10.10_spmd, body=%wide.region_4.9_spmd.sunk | while | flops 154098560 | bytes 12468941 | solution.py:175
  265.8 1.9 fusion.58
  272.1 1.9 fusion.58
  278.4 1.9 fusion.58
  284.7 1.9 fusion.58
  292.2 5.2 %all-to-all-start.1 = ((bf16[4,256,128]{2,0,1:T(4,128)(2,1)}), bf16[4,256,128]{2,0,1:T(4,128)(2,1)S(1)}, u32[]{:S(2)}, u32[]{:S(2)}) async-start(bf16[4,256,128]{2,0,1:T(4,128)(2,1)} %bitcast.34), calls=%async_computation.1 | async-start | bytes 524288 | tf_op jit(solution)/shard_map/all_to_all | solution.py:180
  297.4 6.5 %all-to-all-done.1 = bf16[4,256,128]{2,0,1:T(4,128)(2,1)S(1)} async-done(((bf16[4,256,128]{2,0,1:T(4,128)(2,1)}), bf16[4,256,128]{2,0,1:T(4,128)(2,1)S(1)}, u32[]{:S(2)}, u32[]{:S(2)}) %all-to-all-start.1) | async-done | bytes 262176 | tf_op jit(solution)/shard_map/all_to_all | solution.py:180
  (433 shorter events, 101.8 us)
Async XLA Ops:
  6.5 34.2 %copy-start = (bf16[32,4096]{1,0:T(8,128)(2,1)S(1)}, bf16[32,4096]{1,0:T(8,128)(2,1)}, u32[]{:S(2)}) copy-start(bf16[32,4096]{1,0:T(8,128)(2,1)} %param.10) | copy-start | bytes 786436
  6.5 149.0 %all-gather.4.cloned.1.call-start = ((), (), s32[]{:S(2)}) async-start(), calls=%async_computation.2 | async-start | bytes 8519680 | tf_op jit(solution)/shard_map/all_gather | solution.py:133
  6.5 11.7 %collective-permute-start = (bf16[32,2,1024]{2,1,0:T(2,128)(2,1)}, bf16[32,2,1024]{2,1,0:T(2,128)(2,1)S(1)}, u32[]{:S(2)}, u32[]{:S(2)}) collective-permute-start(bf16[32,2,1024]{2,1,0:T(2,128)(2,1)} %param.11), channel_id=1, source_target_pairs={{0,1},{1,2},{2,3},{3,4},{4,5},{5,6},{6,7},{7,0},{8,9},{9,10},{10,1... | collective-permute-start | bytes 393224 | tf_op jit(solution)/shard_map/ppermute | solution.py:27
  9.1 13.5 %collective-permute-start.4 = (bf16[32,2,1024]{2,1,0:T(2,128)(2,1)}, bf16[32,2,1024]{2,1,0:T(2,128)(2,1)S(1)}, u32[]{:S(2)}, u32[]{:S(2)}) collective-permute-start(bf16[32,2,1024]{2,1,0:T(2,128)(2,1)} %param.11), channel_id=1, source_target_pairs={{1,0},{2,1},{3,2},{4,3},{5,4},{6,5},{7,6},{0,7},{9,8},{10,9},{11,1... | collective-permute-start | bytes 393224 | tf_op jit(solution)/shard_map/ppermute | solution.py:29
  18.2 3.8 %collective-permute-start.1 = (bf16[32,2,1024]{2,1,0:T(2,128)(2,1)S(1)}, bf16[32,2,1024]{2,1,0:T(2,128)(2,1)S(1)}, u32[]{:S(2)}, u32[]{:S(2)}) collective-permute-start(bf16[32,2,1024]{2,1,0:T(2,128)(2,1)S(1)} %collective-permute-done), channel_id=1, source_target_pairs={{0,1},{1,2},{2,3},{3,4},{4,5},{5,6},{6,7},{7,0},{8,9},{9,10},{10,1... | collective-permute-start | bytes 393224 | tf_op jit(solution)/shard_map/ppermute | solution.py:27
  22.0 5.6 %collective-permute-start.2 = (bf16[32,2,1024]{2,1,0:T(2,128)(2,1)S(1)}, bf16[32,2,1024]{2,1,0:T(2,128)(2,1)S(1)}, u32[]{:S(2)}, u32[]{:S(2)}) collective-permute-start(bf16[32,2,1024]{2,1,0:T(2,128)(2,1)S(1)} %collective-permute-done.1), channel_id=1, source_target_pairs={{0,1},{1,2},{2,3},{3,4},{4,5},{5,6},{6,7},{7,0},{8,9},{9,10},{10,1... | collective-permute-start | bytes 393224 | tf_op jit(solution)/shard_map/ppermute | solution.py:27
  22.7 5.2 %collective-permute-start.5 = (bf16[32,2,1024]{2,1,0:T(2,128)(2,1)S(1)}, bf16[32,2,1024]{2,1,0:T(2,128)(2,1)S(1)}, u32[]{:S(2)}, u32[]{:S(2)}) collective-permute-start(bf16[32,2,1024]{2,1,0:T(2,128)(2,1)S(1)} %collective-permute-done.4), channel_id=1, source_target_pairs={{1,0},{2,1},{3,2},{4,3},{5,4},{6,5},{7,6},{0,7},{9,8},{10,9},{11,1... | collective-permute-start | bytes 393224 | tf_op jit(solution)/shard_map/ppermute | solution.py:29
  27.7 5.6 %collective-permute-start.3 = (bf16[32,2,1024]{2,1,0:T(2,128)(2,1)S(1)}, bf16[32,2,1024]{2,1,0:T(2,128)(2,1)S(1)}, u32[]{:S(2)}, u32[]{:S(2)}) collective-permute-start(bf16[32,2,1024]{2,1,0:T(2,128)(2,1)S(1)} %collective-permute-done.2), channel_id=1, source_target_pairs={{0,1},{1,2},{2,3},{3,4},{4,5},{5,6},{6,7},{7,0},{8,9},{9,10},{10,1... | collective-permute-start | bytes 393224 | tf_op jit(solution)/shard_map/ppermute | solution.py:27
  27.8 7.1 %collective-permute-start.6 = (bf16[32,2,1024]{2,1,0:T(2,128)(2,1)S(1)}, bf16[32,2,1024]{2,1,0:T(2,128)(2,1)S(1)}, u32[]{:S(2)}, u32[]{:S(2)}) collective-permute-start(bf16[32,2,1024]{2,1,0:T(2,128)(2,1)S(1)} %collective-permute-done.5), channel_id=1, source_target_pairs={{1,0},{2,1},{3,2},{4,3},{5,4},{6,5},{7,6},{0,7},{9,8},{10,9},{11,1... | collective-permute-start | bytes 393224 | tf_op jit(solution)/shard_map/ppermute | solution.py:29
  40.0 15.5 %copy-start.1 = (s32[32]{0:T(128)S(1)}, s32[32]{0:T(128)}, u32[]{:S(2)}) copy-start(s32[32]{0:T(128)} %param.15) | copy-start | bytes 388
  40.0 53.3 %copy-start.4 = (s32[32,8]{0,1:T(8,128)S(1)}, s32[32,8]{0,1:T(8,128)}, u32[]{:S(2)}) copy-start(s32[32,8]{0,1:T(8,128)} %param.14) | copy-start | bytes 3076
  41.5 52.5 %collective-permute-start.7 = (bf16[256,2,4,128]{3,0,1,2:T(8,128)(2,1)S(1)}, bf16[256,2,4,128]{3,0,1,2:T(8,128)(2,1)S(1)}, u32[]{:S(2)}, u32[]{:S(2)}) collective-permute-start(bf16[256,2,4,128]{3,0,1,2:T(8,128)(2,1)S(1)} %bitcast_select_fusion), channel_id=1, source_target_pairs={{0,16},{8,24},{16,32},{24,40},{32,48},{40,56},{48,64},{56,72},{64,... | collective-permute-start | bytes 1572872 | tf_op jit(solution)/shard_map/ppermute | solution.py:39
  42.8 51.2 %collective-permute-start.8 = (bf16[256,2,4,128]{3,0,1,2:T(8,128)(2,1)S(1)}, bf16[256,2,4,128]{3,0,1,2:T(8,128)(2,1)S(1)}, u32[]{:S(2)}, u32[]{:S(2)}) collective-permute-start(bf16[256,2,4,128]{3,0,1,2:T(8,128)(2,1)S(1)} %bitcast_select_fusion), channel_id=1, source_target_pairs={{0,8},{8,16},{16,24},{24,32},{32,40},{40,48},{48,56},{56,64},{64,7... | collective-permute-start | bytes 1572872 | tf_op jit(solution)/shard_map/ppermute | solution.py:39
  46.9 47.1 %all-to-all-start = ((bf16[32,32,128]{2,0,1:T(8,128)(2,1)}), bf16[32,32,128]{2,0,1:T(8,128)(2,1)S(1)}, u32[]{:S(2)}, u32[]{:S(2)}) async-start(bf16[32,32,128]{2,0,1:T(8,128)(2,1)} %select_bitcast_fusion), calls=%async_computation | async-start | bytes 524288 | tf_op jit(solution)/shard_map/all_to_all | solution.py:111
  168.0 1.2 copy-start.2
  174.3 1.2 copy-start.2
  180.6 1.2 copy-start.2
  186.9 1.2 copy-start.2
  201.7 1.2 copy-start.2
  207.9 1.2 copy-start.2
  214.2 1.2 copy-start.2
  220.5 1.2 copy-start.2
  235.3 1.2 copy-start.2
  241.6 1.2 copy-start.2
  247.9 1.2 copy-start.2
  254.2 1.2 copy-start.2
  269.0 1.2 copy-start.2
  275.3 1.2 copy-start.2
  281.6 1.2 copy-start.2
  287.9 1.2 copy-start.2
  290.3 14.2 %copy-start.3 = (bf16[32,4096]{1,0:T(8,128)(2,1)S(1)}, bf16[32,4096]{1,0:T(8,128)(2,1)}, u32[]{:S(2)}) copy-start(bf16[32,4096]{1,0:T(8,128)(2,1)} %param.12) | copy-start | bytes 786436
  292.2 11.7 %all-to-all-start.1 = ((bf16[4,256,128]{2,0,1:T(4,128)(2,1)}), bf16[4,256,128]{2,0,1:T(4,128)(2,1)S(1)}, u32[]{:S(2)}, u32[]{:S(2)}) async-start(bf16[4,256,128]{2,0,1:T(4,128)(2,1)} %bitcast.34), calls=%async_computation.1 | async-start | bytes 524288 | tf_op jit(solution)/shard_map/all_to_all | solution.py:180
Sparse Core Ops, SparseCore 0:
  40.8 114.7 all-gather.3
